TPU v7x, 1024 devices: a whole 8x8x8 slice. The times are simulated.
1024 devices in a mesh: batch: 16 (over z, core), proto: 64 (over y, x).
Axes of the slice: x: 8, y: 8, z: 8, core: 2. Of those that a mesh axis runs over, the one named last changes fastest.
Arguments:
- teacher: bfloat16 [64, 256, 256], P('batch'), may hold values from -1 to 1
- student: bfloat16 [64, 256, 256], P('batch'), may hold values from -0.5 to 0.5
- perm: int32 [64, 256], P('batch'), may hold values from 0 to 255, each once within a row
- counts: int32 [16, 4], P('batch'), may hold values from 1 to 128, 384 in all within a row
- prototypes: bfloat16 [256, 131072], P(None, 'proto'), may hold values from -1 to 1
Outputs:
- feature_grad: float32 [6144, 256], P(('batch', 'proto'))
- proto_grad: float32 [256, 131072], P('batch', 'proto')
Inputs may be any that keep to these rules, and one draw needn't show every extreme that they name: Each row of counts sums to exactly 384; some image of each batch index has exactly 128 masked patches. Each row of perm is a permutation of the 256 patches; the first counts entries of an image's row are its masked patches.
All inputs are finite; a program needn't handle non-finite values.
Results may differ from a plain program's by a relative error of at most 0.0053.
Values sent between devices are 32-bit elements; how exact they have to be, the bound alone decides.
No kernel may reach another device: no remote copies, remote signals or barrier semaphores. Data moves between devices by JAX's collectives and lax.ppermute only.
A program may use at most 32 MiB of HBM per device.

v0:
```python
import jax
import jax.numpy as jnp
from jax import lax
from jax.sharding import PartitionSpec as P

K = 131072
SWEEPS = 3
GROUP_ROWS = 384


def sent_to_all(shard, axis):
    length = lax.axis_size(axis)
    return lax.all_to_all(
        jnp.broadcast_to(shard[None], (length, *shard.shape)), axis, 0, 0, tiled=True
    )


def taken_together(shard, axis):
    everything = sent_to_all(shard, axis)
    return jnp.sum(everything, axis=0)


def packed_total(arrays, axis):
    ravelled, at, finished = (jnp.concatenate([a.reshape(-1) for a in arrays]), 0, [])
    total = taken_together(ravelled, axis)
    for a in arrays:
        finished.append(total[at : at + a.size].reshape(a.shape))
        at += a.size
    return tuple(finished)


def split_up(shard, dim, length):
    lengths = shard.shape
    parts = shard.reshape(*lengths[:dim], length, lengths[dim] // length, *lengths[dim + 1 :])
    return jnp.moveaxis(parts, dim, 0)


def summed_on_arrival(shard, axis, dim):
    parts = split_up(shard, dim, lax.axis_size(axis))
    arrived = lax.all_to_all(parts, axis, split_axis=0, concat_axis=0, tiled=True)
    return arrived.sum(axis=0)


def unit_rows(rows):
    values = rows.astype(jnp.float32)
    inverse = lax.rsqrt(jnp.sum(values * values, axis=1, keepdims=True) + 1e-06)
    return (values * inverse, inverse)


def row_total(partial_value):
    return taken_together(partial_value, "proto")


def on_device(teacher, student, perm, counts, prototypes):
    img_count = teacher.shape[0]
    patches = teacher.shape[1]
    width = teacher.shape[2]
    group_rows = GROUP_ROWS
    tally = counts.reshape(-1)
    ends = jnp.cumsum(tally)
    starts = ends - tally
    line = jnp.arange(group_rows, dtype=jnp.int32)
    owner = jnp.sum((ends[None, :] <= line[:, None]).astype(jnp.int32), axis=1)
    picked = owner[:, None] == jnp.arange(img_count, dtype=jnp.int32)[None, :]
    first = jnp.sum(jnp.where(picked, starts[None, :], 0), axis=1)
    owned = jnp.sum(jnp.where(picked, tally[None, :], 0), axis=1)
    inner = line - first
    packed_patch = jnp.take(perm.reshape(-1), owner * patches + inner)
    packed_flat = owner * patches + packed_patch
    live = jnp.ones((group_rows,), jnp.float32)
    weight_row = 1.0 / owned.astype(jnp.float32)
    teach_flat = teacher.reshape(-1, width)
    stud_flat = student.reshape(-1, width)
    teach_unit, unused = unit_rows(jnp.take(teach_flat, packed_flat, axis=0))
    stud_unit, unused_inv = unit_rows(jnp.take(stud_flat, packed_flat, axis=0))
    teach_half = teach_unit.astype(jnp.bfloat16)
    stud_half = stud_unit.astype(jnp.bfloat16)
    energy = jnp.exp(jnp.dot(teach_half, prototypes, preferred_element_type=jnp.float32) * 25.0)
    expo = jnp.exp(jnp.dot(stud_half, prototypes, preferred_element_type=jnp.float32) * 10.0)
    soft_part = jnp.sum(expo, axis=1)
    soft_total = soft_part
    row_scale = live
    col_scale = jnp.ones((energy.shape[1],), jnp.float32)
    for sweep in range(SWEEPS):
        col_part = jnp.dot(row_scale, energy, precision=lax.Precision.HIGHEST)
        col_scale = 1.0 / taken_together(col_part, "batch")
        row_part = jnp.dot(energy, col_scale, precision=lax.Precision.HIGHEST)
        if sweep == SWEEPS - 1:
            rows_sum, soft_total = packed_total((row_part, soft_part), "proto")
        else:
            rows_sum = row_total(row_part)
        row_scale = live / rows_sum
    soft = expo / soft_total[:, None]
    target = row_scale[:, None] * energy * col_scale[None, :]
    grad = (K * 10.0 * weight_row[:, None] * (soft - target)).astype(jnp.bfloat16)
    proto_grad = summed_on_arrival(
        lax.dot_general(
            stud_half, grad, (((0,), (0,)), ((), ())), preferred_element_type=jnp.float32
        ),
        "batch",
        0,
    )
    share = group_rows // lax.axis_size("proto")
    back = summed_on_arrival(
        lax.dot_general(
            grad, prototypes, (((1,), (1,)), ((), ())), preferred_element_type=jnp.float32
        ),
        "proto",
        0,
    )
    begin = lax.axis_index("proto") * share
    mine = lax.dynamic_slice_in_dim(packed_flat, begin, share, 0)
    own_unit, own_inverse = unit_rows(jnp.take(stud_flat, mine, axis=0))
    feature_grad = own_inverse * (back - own_unit * jnp.sum(own_unit * back, axis=1, keepdims=True))
    return (feature_grad, proto_grad)


def solution(mesh):
    in_specs = (
        P("batch", None, None),
        P("batch", None, None),
        P("batch", None),
        P("batch", None),
        P(None, "proto"),
    )
    out_specs = (P(("batch", "proto"), None), P("batch", "proto"))
    return jax.shard_map(
        on_device, mesh=mesh, in_specs=in_specs, out_specs=out_specs, check_vma=False
    )
```

profile of v0, /device:TPU:1, one launch (start us, length us, event | category | flops | bytes accessed | tf_op | source)
XLA Modules:
  0.0 233.0 jit_solution(4758510817344071491)
XLA Ops:
  0.7 1.0 reduce-window.4
  3.9 1.9 gather_fusion
  5.8 2.1 gather_fusion.2
  7.9 2.1 gather_fusion.3
  10.9 1.7 copy-done.1
  12.6 1.6 fusion.13
  14.3 26.9 %all_to_all.46 = f32[16,1,2048]{2,1,0:T(1,128)S(1)} all-to-all(f32[16,1,2048]{2,1,0:T(1,128)S(1)} %broadcast_in_dim.107), channel_id=1, replica_groups=mesh['batch'=16,'proto'=64] {'batch'}, dimensions={0} | all-to-all | bytes 262144 | tf_op jit(solution)/shard_map/all_to_all | solution.py:13
  41.2 4.6 %convolution_reduce_fusion.2 = f32[384]{0:T(512)S(1)} fusion(f32[384,2048]{1,0:T(8,128)} %copy-done.1, f32[2048,1]{0,1:T(1,128)S(1)} %bitcast.45), kind=kOutput, calls=%fused_computation.9 | convolution fusion | flops 9437184 | bytes 3155456 | tf_op jit(solution)/shard_map/dot_general | solution.py:87
  45.9 24.4 %all_to_all.47 = f32[64,1,384]{2,1,0:T(1,128)S(1)} all-to-all(f32[64,1,384]{2,1,0:T(1,128)S(1)} %broadcast_in_dim.108), channel_id=1, replica_groups=mesh['batch'=16,'proto'=64] {'proto'}, dimensions={0} | all-to-all | bytes 196608 | tf_op jit(solution)/shard_map/all_to_all | solution.py:13
  70.4 3.5 %fusion.23 = f32[1,2048]{1,0:T(1,128)S(1)} fusion(f32[384,1]{0,1:T(1,128)S(1)} %reshape.196, f32[384,2048]{1,0:T(8,128)} %copy-done.1), kind=kOutput, calls=%fused_computation.67 | convolution fusion | flops 9437184 | bytes 3155456 | tf_op jit(solution)/shard_map/dot_general | solution.py:85
  73.9 13.2 %all_to_all.48 = f32[16,1,2048]{2,1,0:T(1,128)S(1)} all-to-all(f32[16,1,2048]{2,1,0:T(1,128)S(1)} %broadcast_in_dim.109), channel_id=1, replica_groups=mesh['batch'=16,'proto'=64] {'batch'}, dimensions={0} | all-to-all | bytes 262144 | tf_op jit(solution)/shard_map/all_to_all | solution.py:13
  87.2 4.6 %convolution_reduce_fusion.1 = f32[384]{0:T(512)S(1)} fusion(f32[384,2048]{1,0:T(8,128)} %copy-done.1, f32[2048,1]{0,1:T(1,128)S(1)} %bitcast.46), kind=kOutput, calls=%fused_computation.8 | convolution fusion | flops 9437184 | bytes 3155456 | tf_op jit(solution)/shard_map/dot_general | solution.py:87
  91.9 15.7 %all_to_all.49 = f32[64,1,384]{2,1,0:T(1,128)S(1)} all-to-all(f32[64,1,384]{2,1,0:T(1,128)S(1)} %broadcast_in_dim.110), channel_id=1, replica_groups=mesh['batch'=16,'proto'=64] {'proto'}, dimensions={0} | all-to-all | bytes 196608 | tf_op jit(solution)/shard_map/all_to_all | solution.py:13
  107.6 3.5 %fusion.24 = f32[1,2048]{1,0:T(1,128)S(1)} fusion(f32[384,1]{0,1:T(1,128)S(1)} %reshape.200, f32[384,2048]{1,0:T(8,128)} %copy-done.1), kind=kOutput, calls=%fused_computation.68 | convolution fusion | flops 9437184 | bytes 3155456 | tf_op jit(solution)/shard_map/dot_general | solution.py:85
  111.9 4.2 %all-to-all-start.4 = ((f32[16,1,2048]{2,1,0:T(1,128)}), f32[16,1,2048]{2,1,0:T(1,128)S(1)}, u32[]{:S(2)}, u32[]{:S(2)}) async-start(f32[16,1,2048]{2,1,0:T(1,128)} %broadcast_in_dim.111), calls=%async_computation.4 | async-start | bytes 262144 | tf_op jit(solution)/shard_map/all_to_all | solution.py:13
  116.0 2.4 %fusion.22 = (f32[384]{0:T(512)S(1)}, f32[384,2048]{1,0:T(8,128)}) fusion(bf16[256,2048]{1,0:T(8,128)(2,1)S(1)} %copy-done, f32[384]{0:T(512)S(1)} %get-tuple-element.16, bf16[384,256]{1,0:T(8,128)(2,1)S(1)} %gather_fusion.2, pred[384]{0:T(512)(128)(4,1)S(1)} %get-tuple-element.9), kind=kOutput, calls=%fused_computation.66 | convolution fusion | flops 404618880 | bytes 4394368 | tf_op jit(solution)/shard_map/dot_general | solution.py:79
  118.4 6.8 %all-to-all-done.4 = f32[16,1,2048]{2,1,0:T(1,128)S(1)} async-done(((f32[16,1,2048]{2,1,0:T(1,128)}), f32[16,1,2048]{2,1,0:T(1,128)S(1)}, u32[]{:S(2)}, u32[]{:S(2)}) %all-to-all-start.4) | async-done | bytes 131104 | tf_op jit(solution)/shard_map/all_to_all | solution.py:13
  125.3 4.6 %convolution_reduce_fusion = f32[384]{0:T(512)S(1)} fusion(f32[384,2048]{1,0:T(8,128)} %copy-done.1, f32[2048,1]{0,1:T(1,128)S(1)} %bitcast.41), kind=kOutput, calls=%fused_computation.7 | convolution fusion | flops 9437184 | bytes 3155456 | tf_op jit(solution)/shard_map/dot_general | solution.py:87
  129.9 0.8 broadcast_in_dim.112
  130.7 4.6 %all-to-all-start.5 = ((f32[64,1,768]{2,1,0:T(1,128)}), f32[64,1,768]{2,1,0:T(1,128)S(1)}, u32[]{:S(2)}, u32[]{:S(2)}) async-start(f32[64,1,768]{2,1,0:T(1,128)} %broadcast_in_dim.112), calls=%async_computation.5 | async-start | bytes 393216 | tf_op jit(solution)/shard_map/all_to_all | solution.py:13
  135.3 13.2 %all-to-all-done.5 = f32[64,1,768]{2,1,0:T(1,128)S(1)} async-done(((f32[64,1,768]{2,1,0:T(1,128)}), f32[64,1,768]{2,1,0:T(1,128)S(1)}, u32[]{:S(2)}, u32[]{:S(2)}) %all-to-all-start.5) | async-done | bytes 196640 | tf_op jit(solution)/shard_map/all_to_all | solution.py:13
  148.6 3.5 %multiply_convert_fusion = bf16[384,2048]{1,0:T(8,128)(2,1)S(1)} fusion(f32[384,2048]{1,0:T(8,128)} %copy-done.1, f32[384,2048]{1,0:T(8,128)} %get-tuple-element.14, f32[2048]{0:T(1024)S(1)} %broadcast_divide_fusion, f32[384]{0:T(512)S(1)} %get-tuple-element.12, f32[384]{0:T(512)S(1)} %get-tuple-element.11, f32[384]{0:T(512)S(1)} %divide_multiply_fusion), kind=kLoop, calls=%fused_computation.4 | loop fusion | flops 4718592 | bytes 7877120 | tf_op jit(solution)/shard_map/convert_element_type | solution.py:95
  152.8 0.8 reshape.151
  153.6 4.6 %all-to-all-start.6 = ((f32[64,6,256]{2,1,0:T(8,128)}), f32[64,6,256]{2,1,0:T(8,128)S(1)}, u32[]{:S(2)}, u32[]{:S(2)}) async-start(f32[64,6,256]{2,1,0:T(8,128)} %reshape.151), calls=%async_computation.6 | async-start | bytes 1048576 | tf_op jit(solution)/shard_map/all_to_all | solution.py:40
  158.3 2.2 fusion.18
  160.5 15.1 %all-to-all-done.6 = f32[64,6,256]{2,1,0:T(8,128)S(1)} async-done(((f32[64,6,256]{2,1,0:T(8,128)}), f32[64,6,256]{2,1,0:T(8,128)S(1)}, u32[]{:S(2)}, u32[]{:S(2)}) %all-to-all-start.6) | async-done | bytes 393248 | tf_op jit(solution)/shard_map/all_to_all | solution.py:40
  175.6 0.8 copy-done.4
  176.4 6.7 %all-to-all-start.7 = ((f32[16,16,2048]{2,1,0:T(8,128)}), f32[16,16,2048]{2,1,0:T(8,128)S(1)}, u32[]{:S(2)}, u32[]{:S(2)}) async-start(f32[16,16,2048]{2,1,0:T(8,128)} %bitcast.37), calls=%async_computation.7 | async-start | bytes 4194304 | tf_op jit(solution)/shard_map/all_to_all | solution.py:40
  183.2 1.7 gather_fusion.1
  185.1 1.1 reduce_sum.160
  187.0 45.2 %all-to-all-done.7 = f32[16,16,2048]{2,1,0:T(8,128)S(1)} async-done(((f32[16,16,2048]{2,1,0:T(8,128)}), f32[16,16,2048]{2,1,0:T(8,128)S(1)}, u32[]{:S(2)}, u32[]{:S(2)}) %all-to-all-start.7) | async-done | bytes 2097184 | tf_op jit(solution)/shard_map/all_to_all | solution.py:40
  232.2 0.8 reduce_sum.162
  (49 shorter events, 6.6 us)
Async XLA Ops:
  0.6 9.6 %copy-start = (bf16[256,2048]{1,0:T(8,128)(2,1)S(1)}, bf16[256,2048]{1,0:T(8,128)(2,1)}, u32[]{:S(2)}) copy-start(bf16[256,2048]{1,0:T(8,128)(2,1)} %param.11) | copy-start | bytes 3145732
  0.6 5.2 %copy-start.2 = (bf16[4,256,256]{2,1,0:T(8,128)(2,1)S(1)}, bf16[4,256,256]{2,1,0:T(8,128)(2,1)}, u32[]{:S(2)}) copy-start(bf16[4,256,256]{2,1,0:T(8,128)(2,1)} %param.8) | copy-start | bytes 1572868
  0.7 7.2 %copy-start.3 = (bf16[4,256,256]{2,1,0:T(8,128)(2,1)S(1)}, bf16[4,256,256]{2,1,0:T(8,128)(2,1)}, u32[]{:S(2)}) copy-start(bf16[4,256,256]{2,1,0:T(8,128)(2,1)} %param.7) | copy-start | bytes 1572868
  10.9 1.7 copy-start.1
  111.9 13.4 %all-to-all-start.4 = ((f32[16,1,2048]{2,1,0:T(1,128)}), f32[16,1,2048]{2,1,0:T(1,128)S(1)}, u32[]{:S(2)}, u32[]{:S(2)}) async-start(f32[16,1,2048]{2,1,0:T(1,128)} %broadcast_in_dim.111), calls=%async_computation.4 | async-start | bytes 262144 | tf_op jit(solution)/shard_map/all_to_all | solution.py:13
  130.7 17.8 %all-to-all-start.5 = ((f32[64,1,768]{2,1,0:T(1,128)}), f32[64,1,768]{2,1,0:T(1,128)S(1)}, u32[]{:S(2)}, u32[]{:S(2)}) async-start(f32[64,1,768]{2,1,0:T(1,128)} %broadcast_in_dim.112), calls=%async_computation.5 | async-start | bytes 393216 | tf_op jit(solution)/shard_map/all_to_all | solution.py:13
  153.6 22.0 %all-to-all-start.6 = ((f32[64,6,256]{2,1,0:T(8,128)}), f32[64,6,256]{2,1,0:T(8,128)S(1)}, u32[]{:S(2)}, u32[]{:S(2)}) async-start(f32[64,6,256]{2,1,0:T(8,128)} %reshape.151), calls=%async_computation.6 | async-start | bytes 1048576 | tf_op jit(solution)/shard_map/all_to_all | solution.py:40
  175.6 0.8 copy-start.4
  176.4 55.8 %all-to-all-start.7 = ((f32[16,16,2048]{2,1,0:T(8,128)}), f32[16,16,2048]{2,1,0:T(8,128)S(1)}, u32[]{:S(2)}, u32[]{:S(2)}) async-start(f32[16,16,2048]{2,1,0:T(8,128)} %bitcast.37), calls=%async_computation.7 | async-start | bytes 4194304 | tf_op jit(solution)/shard_map/all_to_all | solution.py:40
where the time goes:
time: 234 us; the launch traced here: 233 us
  waiting for transfers between devices  80.2 us (34%)
  blocking collectives  80.1 us (34%)
  matrix products  28.1 us (12%)
  starting transfers between devices  20.2 us (9%)
  local copies, waits for them, and re-layouts  13.4 us (6%)
  other arithmetic  10 us (4%)
    all_to_all x4, blocking collectives, sent_to_all(): lax.all_to_all(jnp.broadcast_to(shard[None], (length, *shard.shape)), axi...  80.1 us
    all_to_all x2, waiting for transfers between devices, summed_on_arrival(): lax.all_to_all(parts, axis, split_axis=0, concat_axis=0, tiled=True)  60.3 us
    all_to_all x2, waiting for transfers between devices, sent_to_all(): lax.all_to_all(jnp.broadcast_to(shard[None], (length, *shard.shape)), axi...  19.9 us
    dot_general x3, matrix products, on_device(): row_part = jnp.dot(energy, col_scale, precision=lax.Precision.HIGHEST)  13.7 us
    all_to_all x2, starting transfers between devices, summed_on_arrival(): lax.all_to_all(parts, axis, split_axis=0, concat_axis=0, tiled=True)  11.4 us
    all_to_all x2, starting transfers between devices, sent_to_all(): lax.all_to_all(jnp.broadcast_to(shard[None], (length, *shard.shape)), axi...  8.79 us
    dot_general x3, matrix products, on_device(): col_part = jnp.dot(row_scale, energy, precision=lax.Precision.HIGHEST)  8.54 us
  transfers between devices with their start and end apart: 4, of which 4 were waited for; matrix products, arithmetic and copies ran while one was open for 4% of the time, Pallas kernels for 0%

commit v1 on v0

v1 whole, which is shorter than its diff:
```python
import jax
import jax.numpy as jnp
from jax import lax
from jax.experimental import pallas as pl
from jax.experimental.pallas import tpu as pltpu
from jax.sharding import PartitionSpec as P

K = 131072
SWEEPS = 3
ROWS = 384
BOT = 256
COLS = 2048
PATCHES = 256
IMAGES = 4
HALF = COLS // 2
LANES = 128
NB = 16
NP = 64
NZ = 8
F32 = jnp.float32
BF16 = jnp.bfloat16


def unit_rows(values):
    inverse = lax.rsqrt(jnp.sum(values * values, axis=1, keepdims=True) + 1e-06)
    return values * inverse, inverse


def to_column(line):
    return jnp.broadcast_to(line, (LANES, ROWS)).T


def to_line(part):
    return jnp.sum(part.T, axis=0, keepdims=True)


def tile_sums(part):
    return jnp.concatenate([jnp.sum(p, axis=0, keepdims=True) for p in part], axis=0)


def start_body(counts, core, perm, teacher, student, protos, energy, col_out, rows_out, hs_out, keep_out, send_out, weight_out, ht):
    @pl.when(pl.program_id(0) == 0)
    def _():
        row = lax.broadcasted_iota(jnp.int32, (ROWS, PATCHES), 0)
        place = lax.broadcasted_iota(jnp.int32, (ROWS, PATCHES), 1)
        row_line = lax.broadcasted_iota(jnp.int32, (ROWS, LANES), 0)
        found = jnp.zeros((ROWS, PATCHES), F32)
        owned = jnp.zeros((ROWS, LANES), F32)
        begin = jnp.int32(0)
        for m in range(IMAGES):
            tally = counts[0, m]
            inner = row - begin
            hit = (inner == place) & (place < tally)
            label = (perm[m : m + 1, :] + m * PATCHES).astype(F32)
            found = found + jnp.where(hit, label, 0.0)
            mine = (row_line >= begin) & (row_line < begin + tally)
            owned = owned + jnp.where(mine, tally.astype(F32), 0.0)
            begin = begin + tally
        flat = jnp.sum(found, axis=1, keepdims=True).astype(jnp.int32)
        weight_out[...] = 1.0 / owned
        choice = lax.broadcasted_iota(jnp.int32, (ROWS, IMAGES * PATCHES), 1) == flat
        choice = jnp.where(choice, 1.0, 0.0).astype(BF16)
        t_rows = jnp.dot(choice, teacher[...].reshape(IMAGES * PATCHES, BOT), preferred_element_type=F32)
        ht[...] = unit_rows(t_rows)[0].astype(BF16)
        s_rows = jnp.dot(choice, student[...].reshape(IMAGES * PATCHES, BOT), preferred_element_type=F32)
        rows_out[...] = s_rows
        zs = unit_rows(s_rows)[0]
        hs_out[...] = zs.astype(BF16)
        turned = zs.T.reshape(NZ, 2, NB, ROWS)
        even = turned[:, 0].reshape(BOT // 2, ROWS)
        odd = turned[:, 1].reshape(BOT // 2, ROWS)
        first = core[0] == 0
        keep_out[...] = jnp.where(first, even, odd).astype(BF16)
        send_out[...] = jnp.where(first, odd, even).astype(BF16)

    sums = []
    for c in range(HALF // 256):
        at = slice(c * 256, (c + 1) * 256)
        e = jnp.exp(jnp.dot(ht[...], protos[:, at], preferred_element_type=F32) * 25.0)
        energy[:, at] = e
        sums += [e[:, :LANES], e[:, LANES:]]
    col_out[...] = jnp.broadcast_to(tile_sums(sums)[None], (NB, HALF // LANES, LANES))


def soft_body(hs, protos, out, acc):
    step = pl.program_id(0)
    part = jnp.zeros((ROWS, LANES), F32)
    for c in range(HALF // 256):
        at = slice(c * 256, (c + 1) * 256)
        e = jnp.exp(jnp.dot(hs[...], protos[:, at], preferred_element_type=F32) * 10.0)
        part = part + e[:, :LANES] + e[:, LANES:]

    @pl.when(step == 0)
    def _():
        acc[...] = part

    @pl.when(step == 1)
    def _():
        out[...] = to_line(acc[...] + part)


def row_work(cols, energy, acc):
    scale = 1.0 / jnp.sum(cols[...], axis=0)
    part = jnp.zeros((ROWS, LANES), F32)
    for j in range(HALF // LANES):
        part = part + energy[:, j * LANES : (j + 1) * LANES] * scale[j : j + 1, :]

    @pl.when(pl.program_id(0) == 0)
    def _():
        acc[...] = part

    return part


def row_body(cols, energy, out, acc):
    part = row_work(cols, energy, acc)

    @pl.when(pl.program_id(0) == 1)
    def _():
        out[...] = jnp.broadcast_to(to_line(acc[...] + part)[None], (NP, 1, ROWS))


def row_soft_body(cols, energy, soft, out, acc):
    part = row_work(cols, energy, acc)

    @pl.when(pl.program_id(0) == 1)
    def _():
        line = jnp.concatenate([to_line(acc[...] + part), soft[...]], axis=1)
        out[...] = jnp.broadcast_to(line[None], (NP, 1, 2 * ROWS))


def col_body(rows, energy, out, scale):
    @pl.when(pl.program_id(0) == 0)
    def _():
        scale[...] = to_column(1.0 / jnp.sum(rows[:, :, :ROWS], axis=0))

    s = scale[...]
    sums = [energy[:, j * LANES : (j + 1) * LANES] * s for j in range(HALF // LANES)]
    out[...] = jnp.broadcast_to(tile_sums(sums)[None], (NB, HALF // LANES, LANES))


def grad_body(rows, softs, cols, energy, hs, hk, hx, weight, protos, keep, send, back, row_scale, soft_scale):
    step = pl.program_id(0)

    @pl.when(step == 0)
    def _():
        row_scale[...] = to_column(1.0 / jnp.sum(rows[...], axis=0))
        soft_scale[...] = to_column(1.0 / jnp.sum(softs[:, :, ROWS:], axis=0))
        back[...] = jnp.zeros((ROWS, BOT), F32)

    col_scale = 1.0 / jnp.sum(cols[...], axis=0)
    rs = row_scale[...]
    ss = soft_scale[...]
    factor = weight[...] * (K * 10.0)
    total = back[...]
    for c in range(HALF // 256):
        at = slice(c * 256, (c + 1) * 256)
        block = protos[:, at]
        expo = jnp.exp(jnp.dot(hs[...], block, preferred_element_type=F32) * 10.0)
        parts = []
        for h in range(2):
            j = 2 * c + h
            lane = slice(j * LANES, (j + 1) * LANES)
            soft = expo[:, h * LANES : (h + 1) * LANES] * ss
            target = rs * energy[:, lane] * col_scale[j : j + 1, :]
            parts.append((factor * (soft - target)).astype(BF16))
        g = jnp.concatenate(parts, axis=1)
        keep[:, :, at] = jnp.dot(hk[...], g, preferred_element_type=F32).reshape(NZ, NB, 256)
        send[:, :, at] = jnp.dot(hx[...], g, preferred_element_type=F32).reshape(NZ, NB, 256)
        total = total + lax.dot_general(g, block, (((1,), (1,)), ((), ())), preferred_element_type=F32)
    back[...] = total


def whole(shape):
    return pl.BlockSpec(shape, lambda i: (0,) * len(shape))


ENERGY = pl.BlockSpec((ROWS, HALF), lambda i: (0, i))
PROTOS = pl.BlockSpec((BOT, HALF), lambda i: (0, i))
COL = pl.BlockSpec((NB, HALF // LANES, LANES), lambda i: (0, i, 0))
COL_SHAPE = jax.ShapeDtypeStruct((NB, COLS // LANES, LANES), F32)
SMEM = pl.BlockSpec(memory_space=pltpu.SMEM)
PARAMS = pltpu.CompilerParams(dimension_semantics=("arbitrary",))


def call(body, name, ins, outs, shapes, scratch):
    return pl.pallas_call(
        body, grid=(2,), in_specs=ins, out_specs=outs, out_shape=shapes,
        scratch_shapes=scratch, compiler_params=PARAMS, name=name,
    )


def shape(dims, dtype=F32):
    return jax.ShapeDtypeStruct(dims, dtype)


def exchange(sent, axis):
    return lax.all_to_all(sent, axis, 0, 0, tiled=True)


def on_device(teacher, student, perm, counts, protos):
    member = lax.axis_index("batch")
    core = (member % 2).astype(jnp.int32).reshape(1)
    energy, col_sent, rows, hs, hk, hx, weight = call(
        start_body, "start",
        [SMEM, SMEM, whole((IMAGES, PATCHES)), whole((IMAGES, PATCHES, BOT)), whole((IMAGES, PATCHES, BOT)), PROTOS],
        [ENERGY, COL, whole((ROWS, BOT)), whole((ROWS, BOT)), whole((BOT // 2, ROWS)), whole((BOT // 2, ROWS)), whole((ROWS, LANES))],
        [shape((ROWS, COLS)), COL_SHAPE, shape((ROWS, BOT)), shape((ROWS, BOT), BF16), shape((BOT // 2, ROWS), BF16),
         shape((BOT // 2, ROWS), BF16), shape((ROWS, LANES))],
        [pltpu.VMEM((ROWS, BOT), BF16)],
    )(counts, core, perm, teacher, student, protos)
    soft_line = call(
        soft_body, "soft", [whole((ROWS, BOT)), PROTOS], whole((1, ROWS)), shape((1, ROWS)), [pltpu.VMEM((ROWS, LANES), F32)]
    )(hs, protos)
    column = pltpu.VMEM((ROWS, LANES), F32)
    softs = None
    for sweep in range(SWEEPS):
        cols = exchange(col_sent, "batch")
        if sweep == 0:
            sent = call(
                row_soft_body, "rowsoft", [COL, ENERGY, whole((1, ROWS))], whole((NP, 1, 2 * ROWS)),
                shape((NP, 1, 2 * ROWS)), [column],
            )(cols, energy, soft_line)
        else:
            sent = call(row_body, "row", [COL, ENERGY], whole((NP, 1, ROWS)), shape((NP, 1, ROWS)), [column])(cols, energy)
        got = exchange(sent, "proto")
        if sweep == 0:
            softs = got
        if sweep < SWEEPS - 1:
            col_sent = call(col_body, "col", [whole(got.shape), ENERGY], COL, COL_SHAPE, [column])(got, energy)
    piece = pl.BlockSpec((NZ, NB, HALF), lambda i: (0, 0, i))
    keep, send, back = call(
        grad_body, "grad",
        [whole((NP, 1, ROWS)), whole((NP, 1, 2 * ROWS)), COL, ENERGY, whole((ROWS, BOT)), whole((BOT // 2, ROWS)),
         whole((BOT // 2, ROWS)), whole((ROWS, LANES)), PROTOS],
        [piece, piece, whole((ROWS, BOT))],
        [shape((NZ, NB, COLS)), shape((NZ, NB, COLS)), shape((ROWS, BOT))],
        [column, column],
    )(got, softs, cols, energy, hs, hk, hx, weight, protos)
    swap = [(b, b ^ 1) for b in range(NB)]
    share = ROWS // NP
    back_got = exchange(back.reshape(NP, share, BOT), "proto")
    pair = keep + lax.ppermute(send, "batch", swap)
    ring = [list(range(c, NB, 2)) for c in range(2)]
    proto_grad = lax.all_to_all(pair, "batch", 0, 0, axis_index_groups=ring, tiled=True).sum(axis=0)
    mine = lax.dynamic_slice_in_dim(rows, lax.axis_index("proto") * share, share, 0)
    unit, inverse = unit_rows(mine)
    back_sum = back_got.sum(axis=0)
    feature_grad = inverse * (back_sum - unit * jnp.sum(unit * back_sum, axis=1, keepdims=True))
    return (feature_grad, proto_grad)


def solution(mesh):
    in_specs = (
        P("batch", None, None),
        P("batch", None, None),
        P("batch", None),
        P("batch", None),
        P(None, "proto"),
    )
    out_specs = (P(("batch", "proto"), None), P("batch", "proto"))
    return jax.shard_map(
        on_device, mesh=mesh, in_specs=in_specs, out_specs=out_specs, check_vma=False
    )
```

time: 234 us -> 206 us (0.88)
  waiting for transfers between devices: 80.2 us -> 47.7 us
  Pallas kernels: 0 us -> 28.7 us
  matrix products: 28.1 us -> 0 us
  local copies, waits for them, and re-layouts: 13.4 us -> 2.52 us
  blocking collectives: 80.1 us -> 89.6 us
  starting transfers between devices: 20.2 us -> 29.2 us
  other arithmetic: 10 us -> 6.28 us
    all_to_all x4 -> x3, waiting for transfers between devices: 80.2 us -> 47.7 us  [the longest x1 25.9 us: on_device(): lax.all_to_all(pair, 'batch', 0, 0, axis_index_groups=ring, tiled=True)]
    pallas_call x0 -> x8, Pallas kernels: none -> 28.7 us  [the longest x1 6.65 us: on_device(): call(grad_body, 'grad', [whole((NP, 1, ROWS)), whole((NP, 1, 2 * ROWS)),...]
    dot_general x10 -> x0, matrix products: 28.1 us -> none  [the longest x3 13.7 us: on_device(): row_part = jnp.dot(energy, col_scale, precision=lax.Precision.HIGHEST)]
    all_to_all x4 -> x5, blocking collectives: 80.1 us -> 89.6 us  [exchange(): return lax.all_to_all(sent, axis, 0, 0, tiled=True)]
    gather x4 -> x0, local copies, waits for them, and re-layouts: 7.66 us -> none  [the longest x1 2.06 us: on_device(): teach_unit, unused = unit_rows(jnp.take(teach_flat, packed_flat, axis=0))]
    all_to_all x4 -> x3, starting transfers between devices: 20.2 us -> 26.4 us  [the longest x2 22.8 us: exchange(): return lax.all_to_all(sent, axis, 0, 0, tiled=True)]
    convert_element_type x1 -> x0, other arithmetic: 3.51 us -> none  [on_device(): (K * 10.0 * weight_row[:, None] * (soft - target)).astype(jnp.bfloat16)]
    ppermute x0 -> x1, starting transfers between devices: none -> 2.78 us  [on_device(): pair = keep + lax.ppermute(send, 'batch', swap)]
  transfers between devices with their start and end apart: 4 -> 4, of which waited for: 4 -> 3; matrix products, arithmetic and copies ran while one was open for 4% -> 4% of each run, Pallas kernels for 0% -> 1%
where the time goes in v1:
time: 206 us; the launch traced here: 205 us
  blocking collectives  89.6 us (43%)
  waiting for transfers between devices  47.7 us (23%)
  starting transfers between devices  29.2 us (14%)
  Pallas kernels  28.7 us (14%)
  other arithmetic  6.28 us (3%)
  local copies, waits for them, and re-layouts  2.52 us (1%)
    all_to_all x5, blocking collectives, exchange(): return lax.all_to_all(sent, axis, 0, 0, tiled=True)  89.6 us
    all_to_all x1, waiting for transfers between devices, on_device(): lax.all_to_all(pair, 'batch', 0, 0, axis_index_groups=ring, tiled=True)  25.9 us
    all_to_all x2, starting transfers between devices, exchange(): return lax.all_to_all(sent, axis, 0, 0, tiled=True)  22.8 us
    all_to_all x2, waiting for transfers between devices, exchange(): return lax.all_to_all(sent, axis, 0, 0, tiled=True)  21.9 us
    pallas_call x1, Pallas kernels, on_device(): call(grad_body, 'grad', [whole((NP, 1, ROWS)), whole((NP, 1, 2 * ROWS)),...  6.65 us
    pallas_call x2, Pallas kernels, on_device(): call(row_body, 'row', [COL, ENERGY], whole((NP, 1, ROWS)), shape((NP, 1,...  6.02 us
    pallas_call x2, Pallas kernels, on_device(): call(col_body, 'col', [whole(got.shape), ENERGY], COL, COL_SHAPE, [column])  5.57 us
    pallas_call x1, Pallas kernels, on_device(): call(start_body, 'start', [SMEM, SMEM, whole((IMAGES, PATCHES)), whole((I...  4.8 us
  transfers between devices with their start and end apart: 4, of which 3 were waited for; matrix products, arithmetic and copies ran while one was open for 4% of the time, Pallas kernels for 1%

profile of v1, /device:TPU:1, one launch (start us, length us, event | category | flops | bytes accessed | tf_op | source)
XLA Modules:
  0.0 204.7 jit_solution(15926323749454085597)
XLA Ops:
  0.6 4.8 %start.1 = (f32[384,2048]{1,0:T(8,128)}, f32[16,16,128]{2,1,0:T(8,128)}, f32[384,256]{1,0:T(8,128)}, bf16[384,256]{1,0:T(8,128)(2,1)}, bf16[128,384]{1,0:T(8,128...) custom-call(s32[1,4]{1,0:T(1,128)} %counts.1, s32[1]{0:T(128)} %bitcast.core, s32[4,256]{1,0:T(4,128)} %perm.1, ...), custom_call_target="tpu_custom_call" | custom-call | tf_op jit(solution)/shard_map/start/pallas_call | solution.py:204
  5.4 18.2 %all-to-all-start = ((f32[16,16,128]{2,1,0:T(8,128)}), f32[16,16,128]{2,1,0:T(8,128)S(1)}, u32[]{:S(2)}, u32[]{:S(2)}) async-start(f32[16,16,128]{2,1,0:T(8,128)} %get-tuple-element.13), calls=%async_computation | async-start | bytes 262144 | tf_op jit(solution)/shard_map/all_to_all | solution.py:198
  23.6 2.6 %soft.1 = f32[1,384]{1,0:T(1,128)} custom-call(bf16[384,256]{1,0:T(8,128)(2,1)} %get-tuple-element.15.hs, bf16[256,2048]{1,0:T(8,128)(2,1)} %protos.5), custom_call_target="tpu_custom_call" | custom-call | tf_op jit(solution)/shard_map/soft/pallas_call | solution.py:212
  26.2 6.3 %all-to-all-done.cols = f32[16,16,128]{2,1,0:T(8,128)S(1)} async-done(((f32[16,16,128]{2,1,0:T(8,128)}), f32[16,16,128]{2,1,0:T(8,128)S(1)}, u32[]{:S(2)}, u32[]{:S(2)}) %all-to-all-start) | async-done | bytes 131104 | tf_op jit(solution)/shard_map/all_to_all | solution.py:198
  32.5 0.0 copy-start
  32.5 0.7 copy-done
  33.2 3.1 %rowsoft.1 = f32[64,1,768]{2,1,0:T(1,128)} custom-call(f32[16,16,128]{2,1,0:T(8,128)} %copy-done, f32[384,2048]{1,0:T(8,128)} %get-tuple-element.14.energy, f32[1,384]{1,0:T(1,128)} %soft.1), custom_call_target="tpu_custom_call" | custom-call | tf_op jit(solution)/shard_map/rowsoft/pallas_call | solution.py:220
  36.3 26.0 %all_to_all.40.rows.softs = f32[64,1,768]{2,1,0:T(1,128)} all-to-all(f32[64,1,768]{2,1,0:T(1,128)} %rowsoft.1), channel_id=1, replica_groups=mesh['batch'=16,'proto'=64] {'proto'}, dimensions={0} | all-to-all | bytes 393216 | tf_op jit(solution)/shard_map/all_to_all | solution.py:198
  62.3 2.8 %col.2 = f32[16,16,128]{2,1,0:T(8,128)} custom-call(f32[64,1,768]{2,1,0:T(1,128)} %all_to_all.40.rows.softs, f32[384,2048]{1,0:T(8,128)} %get-tuple-element.14.energy), custom_call_target="tpu_custom_call" | custom-call | tf_op jit(solution)/shard_map/col/pallas_call | solution.py:230
  65.1 15.1 %all_to_all.41.cols = f32[16,16,128]{2,1,0:T(8,128)} all-to-all(f32[16,16,128]{2,1,0:T(8,128)} %col.2), channel_id=1, replica_groups=mesh['batch'=16,'proto'=64] {'batch'}, dimensions={0} | all-to-all | bytes 262144 | tf_op jit(solution)/shard_map/all_to_all | solution.py:198
  80.2 3.0 %row.2 = f32[64,1,384]{2,1,0:T(1,128)} custom-call(f32[16,16,128]{2,1,0:T(8,128)} %all_to_all.41.cols, f32[384,2048]{1,0:T(8,128)} %get-tuple-element.14.energy), custom_call_target="tpu_custom_call" | custom-call | tf_op jit(solution)/shard_map/row/pallas_call | solution.py:225
  83.2 17.2 %all_to_all.42.rows = f32[64,1,384]{2,1,0:T(1,128)} all-to-all(f32[64,1,384]{2,1,0:T(1,128)} %row.2), channel_id=1, replica_groups=mesh['batch'=16,'proto'=64] {'proto'}, dimensions={0} | all-to-all | bytes 196608 | tf_op jit(solution)/shard_map/all_to_all | solution.py:198
  100.4 2.8 %col.3 = f32[16,16,128]{2,1,0:T(8,128)} custom-call(f32[64,1,384]{2,1,0:T(1,128)} %all_to_all.42.rows, f32[384,2048]{1,0:T(8,128)} %get-tuple-element.14.energy), custom_call_target="tpu_custom_call" | custom-call | tf_op jit(solution)/shard_map/col/pallas_call | solution.py:230
  103.2 14.0 %all_to_all.43.cols = f32[16,16,128]{2,1,0:T(8,128)} all-to-all(f32[16,16,128]{2,1,0:T(8,128)} %col.3), channel_id=1, replica_groups=mesh['batch'=16,'proto'=64] {'batch'}, dimensions={0} | all-to-all | bytes 262144 | tf_op jit(solution)/shard_map/all_to_all | solution.py:198
  117.2 3.0 %row.3 = f32[64,1,384]{2,1,0:T(1,128)} custom-call(f32[16,16,128]{2,1,0:T(8,128)} %all_to_all.43.cols, f32[384,2048]{1,0:T(8,128)} %get-tuple-element.14.energy), custom_call_target="tpu_custom_call" | custom-call | tf_op jit(solution)/shard_map/row/pallas_call | solution.py:225
  120.2 17.2 %all_to_all.44.rows = f32[64,1,384]{2,1,0:T(1,128)} all-to-all(f32[64,1,384]{2,1,0:T(1,128)} %row.3), channel_id=1, replica_groups=mesh['batch'=16,'proto'=64] {'proto'}, dimensions={0} | all-to-all | bytes 196608 | tf_op jit(solution)/shard_map/all_to_all | solution.py:198
  137.4 6.7 %grad.1 = (f32[8,16,2048]{2,1,0:T(8,128)}, f32[8,16,2048]{2,1,0:T(8,128)}, f32[384,256]{1,0:T(8,128)}) custom-call(f32[64,1,384]{2,1,0:T(1,128)} %all_to_all.44.rows, f32[64,1,768]{2,1,0:T(1,128)} %all_to_all.40.rows.softs, f32[16,16,128]{2,1,0:T(8,128)} %all_to_all.43.cols, f32[384,2048]{1,0:T(8,128)} %get-tuple-element.14.energy, ...), custom_call_target="tpu_custom_call" | custom-call | tf_op jit(solution)/shard_map/grad/pallas_call | solution.py:232
  144.1 2.8 %collective-permute-start = (f32[8,16,2048]{2,1,0:T(8,128)}, f32[8,16,2048]{2,1,0:T(8,128)S(1)}, u32[]{:S(2)}, u32[]{:S(2)}) collective-permute-start(f32[8,16,2048]{2,1,0:T(8,128)} %get-tuple-element.21), channel_id=1, source_target_pairs={{0,64},{64,0},{128,192},{192,128},{256,320},{320,256},{384,448},{4... | collective-permute-start | bytes 3145736 | tf_op jit(solution)/shard_map/ppermute | solution.py:243
  146.9 1.9 reshape.18
  148.7 4.6 %all-to-all-start.6 = ((f32[64,6,256]{2,1,0:T(8,128)}), f32[64,6,256]{2,1,0:T(8,128)S(1)}, u32[]{:S(2)}, u32[]{:S(2)}) async-start(f32[64,6,256]{2,1,0:T(8,128)} %reshape.18), calls=%async_computation.6 | async-start | bytes 1048576 | tf_op jit(solution)/shard_map/all_to_all | solution.py:198
  153.4 0.0 collective-permute-done
  153.4 2.3 %add.21 = f32[8,16,2048]{2,1,0:T(8,128)} add(f32[8,16,2048]{2,1,0:T(8,128)} %get-tuple-element.20, f32[8,16,2048]{2,1,0:T(8,128)S(1)} %collective-permute-done) | non-fusion elementwise | flops 262144 | bytes 3145728 | tf_op jit(solution)/shard_map/add | solution.py:243
  155.7 15.6 %all-to-all-done.6 = f32[64,6,256]{2,1,0:T(8,128)S(1)} async-done(((f32[64,6,256]{2,1,0:T(8,128)}), f32[64,6,256]{2,1,0:T(8,128)S(1)}, u32[]{:S(2)}, u32[]{:S(2)}) %all-to-all-start.6) | async-done | bytes 393248 | tf_op jit(solution)/shard_map/all_to_all | solution.py:198
  171.3 3.6 %all-to-all-start.7 = ((f32[8,16,2048]{2,1,0:T(8,128)}), f32[8,16,2048]{2,1,0:T(8,128)S(1)}, u32[]{:S(2)}, u32[]{:S(2)}) async-start(f32[8,16,2048]{2,1,0:T(8,128)} %add.21), calls=%async_computation.7 | async-start | bytes 2097152 | tf_op jit(solution)/shard_map/all_to_all | solution.py:245
  174.8 0.8 multiply_reduce_fusion.1
  175.7 0.1 reduce_sum.37
  175.8 0.9 multiply_reduce_fusion
  176.7 1.4 subtract_multiply_fusion
  178.1 25.9 %all-to-all-done.7 = f32[8,16,2048]{2,1,0:T(8,128)S(1)} async-done(((f32[8,16,2048]{2,1,0:T(8,128)}), f32[8,16,2048]{2,1,0:T(8,128)S(1)}, u32[]{:S(2)}, u32[]{:S(2)}) %all-to-all-start.7) | async-done | bytes 1048608 | tf_op jit(solution)/shard_map/all_to_all | solution.py:245
  203.9 0.7 reduce_sum.39
  (1 shorter events, 0.0 us)
Async XLA Ops:
  5.4 27.1 %all-to-all-start = ((f32[16,16,128]{2,1,0:T(8,128)}), f32[16,16,128]{2,1,0:T(8,128)S(1)}, u32[]{:S(2)}, u32[]{:S(2)}) async-start(f32[16,16,128]{2,1,0:T(8,128)} %get-tuple-element.13), calls=%async_computation | async-start | bytes 262144 | tf_op jit(solution)/shard_map/all_to_all | solution.py:198
  32.5 0.7 copy-start
  144.1 9.3 %collective-permute-start = (f32[8,16,2048]{2,1,0:T(8,128)}, f32[8,16,2048]{2,1,0:T(8,128)S(1)}, u32[]{:S(2)}, u32[]{:S(2)}) collective-permute-start(f32[8,16,2048]{2,1,0:T(8,128)} %get-tuple-element.21), channel_id=1, source_target_pairs={{0,64},{64,0},{128,192},{192,128},{256,320},{320,256},{384,448},{4... | collective-permute-start | bytes 3145736 | tf_op jit(solution)/shard_map/ppermute | solution.py:243
  148.7 22.5 %all-to-all-start.6 = ((f32[64,6,256]{2,1,0:T(8,128)}), f32[64,6,256]{2,1,0:T(8,128)S(1)}, u32[]{:S(2)}, u32[]{:S(2)}) async-start(f32[64,6,256]{2,1,0:T(8,128)} %reshape.18), calls=%async_computation.6 | async-start | bytes 1048576 | tf_op jit(solution)/shard_map/all_to_all | solution.py:198
  171.3 32.7 %all-to-all-start.7 = ((f32[8,16,2048]{2,1,0:T(8,128)}), f32[8,16,2048]{2,1,0:T(8,128)S(1)}, u32[]{:S(2)}, u32[]{:S(2)}) async-start(f32[8,16,2048]{2,1,0:T(8,128)} %add.21), calls=%async_computation.7 | async-start | bytes 2097152 | tf_op jit(solution)/shard_map/all_to_all | solution.py:245

commit v2 on v1

--- a/solution.py
+++ b/solution.py
@@ -17,6 +17,7 @@
 NB = 16
 NP = 64
 NZ = 8
+SHARE = ROWS // NP
 F32 = jnp.float32
 BF16 = jnp.bfloat16
 
@@ -38,7 +39,7 @@
     return jnp.concatenate([jnp.sum(p, axis=0, keepdims=True) for p in part], axis=0)
 
 
-def start_body(counts, core, perm, teacher, student, protos, energy, col_out, rows_out, hs_out, keep_out, send_out, weight_out, ht):
+def start_body(counts, place_of, perm, teacher, student, protos, energy, col_out, rows_out, hs_out, keep_out, send_out, weight_out, ht):
     @pl.when(pl.program_id(0) == 0)
     def _():
         row = lax.broadcasted_iota(jnp.int32, (ROWS, PATCHES), 0)
@@ -66,12 +67,19 @@
         rows_out[...] = s_rows
         zs = unit_rows(s_rows)[0]
         hs_out[...] = zs.astype(BF16)
-        turned = zs.T.reshape(NZ, 2, NB, ROWS)
-        even = turned[:, 0].reshape(BOT // 2, ROWS)
-        odd = turned[:, 1].reshape(BOT // 2, ROWS)
-        first = core[0] == 0
-        keep_out[...] = jnp.where(first, even, odd).astype(BF16)
-        send_out[...] = jnp.where(first, odd, even).astype(BF16)
+        turned = zs.T.reshape(NZ // 2, 2, 2, NB, ROWS)
+        first = place_of[0] == 0
+        same = place_of[1] == 0
+        kept = []
+        sent = []
+        for z in range(2):
+            low = jnp.where(same, turned[:, z], turned[:, 1 - z])
+            even = low[:, 0].reshape(BOT // 4, ROWS)
+            odd = low[:, 1].reshape(BOT // 4, ROWS)
+            kept.append(jnp.where(first, even, odd))
+            sent.append(jnp.where(first, odd, even))
+        keep_out[...] = jnp.concatenate(kept, axis=0).astype(BF16)
+        send_out[...] = jnp.concatenate(sent, axis=0).astype(BF16)
 
     sums = []
     for c in range(HALF // 256):
@@ -139,7 +147,7 @@
     out[...] = jnp.broadcast_to(tile_sums(sums)[None], (NB, HALF // LANES, LANES))
 
 
-def grad_body(rows, softs, cols, energy, hs, hk, hx, weight, protos, keep, send, back, row_scale, soft_scale):
+def grad_body(rows, softs, cols, energy, hs, hk, hx, weight, protos, near, far, send, back_out, row_scale, soft_scale, back):
     step = pl.program_id(0)
 
     @pl.when(step == 0)
@@ -165,10 +173,17 @@
             target = rs * energy[:, lane] * col_scale[j : j + 1, :]
             parts.append((factor * (soft - target)).astype(BF16))
         g = jnp.concatenate(parts, axis=1)
-        keep[:, :, at] = jnp.dot(hk[...], g, preferred_element_type=F32).reshape(NZ, NB, 256)
+        kept = jnp.dot(hk[...], g, preferred_element_type=F32).reshape(NZ, NB, 256)
+        near[:, :, at] = kept[: NZ // 2]
+        far[:, :, at] = kept[NZ // 2 :]
         send[:, :, at] = jnp.dot(hx[...], g, preferred_element_type=F32).reshape(NZ, NB, 256)
         total = total + lax.dot_general(g, block, (((1,), (1,)), ((), ())), preferred_element_type=F32)
     back[...] = total
+
+    @pl.when(step == 1)
+    def _():
+        for p in range(NP):
+            back_out[p] = back[p * SHARE : (p + 1) * SHARE, :]
 
 
 def whole(shape):
@@ -183,10 +198,10 @@
 PARAMS = pltpu.CompilerParams(dimension_semantics=("arbitrary",))
 
 
-def call(body, name, ins, outs, shapes, scratch):
+def call(body, ins, outs, shapes, scratch):
     return pl.pallas_call(
         body, grid=(2,), in_specs=ins, out_specs=outs, out_shape=shapes,
-        scratch_shapes=scratch, compiler_params=PARAMS, name=name,
+        scratch_shapes=scratch, compiler_params=PARAMS,
     )
 
 
@@ -200,17 +215,17 @@
 
 def on_device(teacher, student, perm, counts, protos):
     member = lax.axis_index("batch")
-    core = (member % 2).astype(jnp.int32).reshape(1)
+    place_of = jnp.stack([member % 2, member // 2 % 2]).astype(jnp.int32)
     energy, col_sent, rows, hs, hk, hx, weight = call(
-        start_body, "start",
+        start_body,
         [SMEM, SMEM, whole((IMAGES, PATCHES)), whole((IMAGES, PATCHES, BOT)), whole((IMAGES, PATCHES, BOT)), PROTOS],
         [ENERGY, COL, whole((ROWS, BOT)), whole((ROWS, BOT)), whole((BOT // 2, ROWS)), whole((BOT // 2, ROWS)), whole((ROWS, LANES))],
         [shape((ROWS, COLS)), COL_SHAPE, shape((ROWS, BOT)), shape((ROWS, BOT), BF16), shape((BOT // 2, ROWS), BF16),
          shape((BOT // 2, ROWS), BF16), shape((ROWS, LANES))],
         [pltpu.VMEM((ROWS, BOT), BF16)],
-    )(counts, core, perm, teacher, student, protos)
+    )(counts, place_of, perm, teacher, student, protos)
     soft_line = call(
-        soft_body, "soft", [whole((ROWS, BOT)), PROTOS], whole((1, ROWS)), shape((1, ROWS)), [pltpu.VMEM((ROWS, LANES), F32)]
+        soft_body, [whole((ROWS, BOT)), PROTOS], whole((1, ROWS)), shape((1, ROWS)), [pltpu.VMEM((ROWS, LANES), F32)]
     )(hs, protos)
     column = pltpu.VMEM((ROWS, LANES), F32)
     softs = None
@@ -218,32 +233,37 @@
         cols = exchange(col_sent, "batch")
         if sweep == 0:
             sent = call(
-                row_soft_body, "rowsoft", [COL, ENERGY, whole((1, ROWS))], whole((NP, 1, 2 * ROWS)),
+                row_soft_body, [COL, ENERGY, whole((1, ROWS))], whole((NP, 1, 2 * ROWS)),
                 shape((NP, 1, 2 * ROWS)), [column],
             )(cols, energy, soft_line)
         else:
-            sent = call(row_body, "row", [COL, ENERGY], whole((NP, 1, ROWS)), shape((NP, 1, ROWS)), [column])(cols, energy)
+            sent = call(row_body, [COL, ENERGY], whole((NP, 1, ROWS)), shape((NP, 1, ROWS)), [column])(cols, energy)
         got = exchange(sent, "proto")
         if sweep == 0:
             softs = got
         if sweep < SWEEPS - 1:
-            col_sent = call(col_body, "col", [whole(got.shape), ENERGY], COL, COL_SHAPE, [column])(got, energy)
+            col_sent = call(col_body, [whole(got.shape), ENERGY], COL, COL_SHAPE, [column])(got, energy)
     piece = pl.BlockSpec((NZ, NB, HALF), lambda i: (0, 0, i))
-    keep, send, back = call(
-        grad_body, "grad",
+    half_piece = pl.BlockSpec((NZ // 2, NB, HALF), lambda i: (0, 0, i))
+    near, far, send, back = call(
+        grad_body,
         [whole((NP, 1, ROWS)), whole((NP, 1, 2 * ROWS)), COL, ENERGY, whole((ROWS, BOT)), whole((BOT // 2, ROWS)),
          whole((BOT // 2, ROWS)), whole((ROWS, LANES)), PROTOS],
-        [piece, piece, whole((ROWS, BOT))],
-        [shape((NZ, NB, COLS)), shape((NZ, NB, COLS)), shape((ROWS, BOT))],
-        [column, column],
+        [half_piece, half_piece, piece, whole((NP, SHARE, BOT))],
+        [shape((NZ // 2, NB, COLS)), shape((NZ // 2, NB, COLS)), shape((NZ, NB, COLS)), shape((NP, SHARE, BOT))],
+        [column, column, pltpu.VMEM((ROWS, BOT), F32)],
     )(got, softs, cols, energy, hs, hk, hx, weight, protos)
     swap = [(b, b ^ 1) for b in range(NB)]
-    share = ROWS // NP
-    back_got = exchange(back.reshape(NP, share, BOT), "proto")
-    pair = keep + lax.ppermute(send, "batch", swap)
-    ring = [list(range(c, NB, 2)) for c in range(2)]
-    proto_grad = lax.all_to_all(pair, "batch", 0, 0, axis_index_groups=ring, tiled=True).sum(axis=0)
-    mine = lax.dynamic_slice_in_dim(rows, lax.axis_index("proto") * share, share, 0)
+    beside = [(b, b ^ 2) for b in range(NB)]
+    swapped = lax.ppermute(send, "batch", swap)
+    back_got = exchange(back, "proto")
+    onward = far + swapped[NZ // 2 :]
+    moved = lax.ppermute(onward, "batch", beside)
+    four = near + swapped[: NZ // 2] + moved
+    groups = [[c + 4 * z for z in range(4)] for c in range(4)]
+    arrived = lax.all_to_all(four, "batch", 0, 0, axis_index_groups=groups, tiled=True)
+    proto_grad = arrived.sum(axis=0)
+    mine = lax.dynamic_slice_in_dim(rows, lax.axis_index("proto") * SHARE, SHARE, 0)
     unit, inverse = unit_rows(mine)
     back_sum = back_got.sum(axis=0)
     feature_grad = inverse * (back_sum - unit * jnp.sum(unit * back_sum, axis=1, keepdims=True))

time: 206 us -> 196 us (0.951)
  the two profiles are of different devices: /device:TPU:1 before, /device:TPU:32 now
where the time goes in v2:
time: 196 us; the launch traced here: 195 us
  blocking collectives  89 us (45%)
  waiting for transfers between devices  37.7 us (19%)
  starting transfers between devices  30.5 us (16%)
  Pallas kernels  28.9 us (15%)
  other arithmetic  7.53 us (4%)
    all_to_all x5, blocking collectives, exchange(): return lax.all_to_all(sent, axis, 0, 0, tiled=True)  89 us
    all_to_all x2, starting transfers between devices, exchange(): return lax.all_to_all(sent, axis, 0, 0, tiled=True)  22.9 us
    all_to_all x2, waiting for transfers between devices, exchange(): return lax.all_to_all(sent, axis, 0, 0, tiled=True)  16.3 us
    all_to_all x1, waiting for transfers between devices, on_device(): lax.all_to_all(four, 'batch', 0, 0, axis_index_groups=groups, tiled=True)  11.1 us
    ppermute x1, waiting for transfers between devices, on_device(): moved = lax.ppermute(onward, 'batch', beside)  7.53 us
    pallas_call x1, Pallas kernels, on_device(): call(grad_body, [whole((NP, 1, ROWS)), whole((NP, 1, 2 * ROWS)), COL, ENE...  6.89 us
    pallas_call x2, Pallas kernels, on_device(): call(row_body, [COL, ENERGY], whole((NP, 1, ROWS)), shape((NP, 1, ROWS)),...  6.02 us
    pallas_call x2, Pallas kernels, on_device(): call(col_body, [whole(got.shape), ENERGY], COL, COL_SHAPE, [column])  5.57 us
  transfers between devices with their start and end apart: 5, of which 5 were waited for; matrix products, arithmetic and copies ran while one was open for 3% of the time, Pallas kernels for 1%

profile of v2, /device:TPU:32, one launch (start us, length us, event | category | flops | bytes accessed | tf_op | source)
XLA Modules:
  0.0 195.0 jit_solution(71805307980072539)
XLA Ops:
  0.7 0.6 pad_add_fusion.place_of
  1.3 4.8 %shard_map.68 = (f32[384,2048]{1,0:T(8,128)}, f32[16,16,128]{2,1,0:T(8,128)}, f32[384,256]{1,0:T(8,128)}, bf16[384,256]{1,0:T(8,128)(2,1)}, bf16[128,384]{1,0:T(...) custom-call(s32[1,4]{1,0:T(1,128)} %counts.1, s32[2]{0:T(128)} %pad_add_fusion.place_of, s32[4,256]{1,0:T(4,128)} %perm.1, ...), custom_call_target="tpu_custom_call" | custom-call | tf_op jit(solution)/shard_map/pallas_call | solution.py:219
  6.0 16.8 %all-to-all-start = ((f32[16,16,128]{2,1,0:T(8,128)}), f32[16,16,128]{2,1,0:T(8,128)S(1)}, u32[]{:S(2)}, u32[]{:S(2)}) async-start(f32[16,16,128]{2,1,0:T(8,128)} %get-tuple-element.14), calls=%async_computation | async-start | bytes 262144 | tf_op jit(solution)/shard_map/all_to_all | solution.py:213
  22.8 2.6 %shard_map.69.soft = f32[1,384]{1,0:T(1,128)} custom-call(bf16[384,256]{1,0:T(8,128)(2,1)} %get-tuple-element.16.hs, bf16[256,2048]{1,0:T(8,128)(2,1)} %protos.5), custom_call_target="tpu_custom_call" | custom-call | tf_op jit(solution)/shard_map/pallas_call | solution.py:227
  25.4 6.1 %all-to-all-done.cols = f32[16,16,128]{2,1,0:T(8,128)S(1)} async-done(((f32[16,16,128]{2,1,0:T(8,128)}), f32[16,16,128]{2,1,0:T(8,128)S(1)}, u32[]{:S(2)}, u32[]{:S(2)}) %all-to-all-start) | async-done | bytes 131104 | tf_op jit(solution)/shard_map/all_to_all | solution.py:213
  31.5 0.7 copy-done
  32.1 3.1 %shard_map.70 = f32[64,1,768]{2,1,0:T(1,128)} custom-call(f32[16,16,128]{2,1,0:T(8,128)} %copy-done, f32[384,2048]{1,0:T(8,128)} %get-tuple-element.15.energy, f32[1,384]{1,0:T(1,128)} %shard_map.69.soft), custom_call_target="tpu_custom_call" | custom-call | tf_op jit(solution)/shard_map/pallas_call | solution.py:235
  35.2 26.6 %all_to_all.40.rows.softs = f32[64,1,768]{2,1,0:T(1,128)} all-to-all(f32[64,1,768]{2,1,0:T(1,128)} %shard_map.70), channel_id=1, replica_groups=mesh['batch'=16,'proto'=64] {'proto'}, dimensions={0} | all-to-all | bytes 393216 | tf_op jit(solution)/shard_map/all_to_all | solution.py:213
  61.8 2.8 %shard_map.71 = f32[16,16,128]{2,1,0:T(8,128)} custom-call(f32[64,1,768]{2,1,0:T(1,128)} %all_to_all.40.rows.softs, f32[384,2048]{1,0:T(8,128)} %get-tuple-element.15.energy), custom_call_target="tpu_custom_call" | custom-call | tf_op jit(solution)/shard_map/pallas_call | solution.py:245
  64.6 12.8 %all_to_all.41.cols = f32[16,16,128]{2,1,0:T(8,128)} all-to-all(f32[16,16,128]{2,1,0:T(8,128)} %shard_map.71), channel_id=1, replica_groups=mesh['batch'=16,'proto'=64] {'batch'}, dimensions={0} | all-to-all | bytes 262144 | tf_op jit(solution)/shard_map/all_to_all | solution.py:213
  77.5 3.0 %shard_map.72 = f32[64,1,384]{2,1,0:T(1,128)} custom-call(f32[16,16,128]{2,1,0:T(8,128)} %all_to_all.41.cols, f32[384,2048]{1,0:T(8,128)} %get-tuple-element.15.energy), custom_call_target="tpu_custom_call" | custom-call | tf_op jit(solution)/shard_map/pallas_call | solution.py:240
  80.5 18.3 %all_to_all.42.rows = f32[64,1,384]{2,1,0:T(1,128)} all-to-all(f32[64,1,384]{2,1,0:T(1,128)} %shard_map.72), channel_id=1, replica_groups=mesh['batch'=16,'proto'=64] {'proto'}, dimensions={0} | all-to-all | bytes 196608 | tf_op jit(solution)/shard_map/all_to_all | solution.py:213
  98.7 2.8 %shard_map.73 = f32[16,16,128]{2,1,0:T(8,128)} custom-call(f32[64,1,384]{2,1,0:T(1,128)} %all_to_all.42.rows, f32[384,2048]{1,0:T(8,128)} %get-tuple-element.15.energy), custom_call_target="tpu_custom_call" | custom-call | tf_op jit(solution)/shard_map/pallas_call | solution.py:245
  101.5 12.8 %all_to_all.43.cols = f32[16,16,128]{2,1,0:T(8,128)} all-to-all(f32[16,16,128]{2,1,0:T(8,128)} %shard_map.73), channel_id=1, replica_groups=mesh['batch'=16,'proto'=64] {'batch'}, dimensions={0} | all-to-all | bytes 262144 | tf_op jit(solution)/shard_map/all_to_all | solution.py:213
  114.3 3.0 %shard_map.74 = f32[64,1,384]{2,1,0:T(1,128)} custom-call(f32[16,16,128]{2,1,0:T(8,128)} %all_to_all.43.cols, f32[384,2048]{1,0:T(8,128)} %get-tuple-element.15.energy), custom_call_target="tpu_custom_call" | custom-call | tf_op jit(solution)/shard_map/pallas_call | solution.py:240
  117.3 18.5 %all_to_all.44.rows = f32[64,1,384]{2,1,0:T(1,128)} all-to-all(f32[64,1,384]{2,1,0:T(1,128)} %shard_map.74), channel_id=1, replica_groups=mesh['batch'=16,'proto'=64] {'proto'}, dimensions={0} | all-to-all | bytes 196608 | tf_op jit(solution)/shard_map/all_to_all | solution.py:213
  135.8 6.9 %shard_map.75 = (f32[4,16,2048]{2,1,0:T(8,128)}, f32[4,16,2048]{2,1,0:T(8,128)}, f32[8,16,2048]{2,1,0:T(8,128)}, f32[64,6,256]{2,1,0:T(8,128)}) custom-call(f32[64,1,384]{2,1,0:T(1,128)} %all_to_all.44.rows, f32[64,1,768]{2,1,0:T(1,128)} %all_to_all.40.rows.softs, f32[16,16,128]{2,1,0:T(8,128)} %all_to_all.43.cols, f32[384,2048]{1,0:T(8,128)} %get-tuple-element.15.energy, ...), custom_call_target="tpu_custom_call" | custom-call | tf_op jit(solution)/shard_map/pallas_call | solution.py:248
  142.7 1.9 collective-permute-start
  144.6 2.8 %collective-permute-done = f32[8,16,2048]{2,1,0:T(8,128)S(1)} collective-permute-done((f32[8,16,2048]{2,1,0:T(8,128)}, f32[8,16,2048]{2,1,0:T(8,128)S(1)}, u32[]{:S(2)}, u32[]{:S(2)}) %collective-permute-start) | collective-permute-done | bytes 1048608 | tf_op jit(solution)/shard_map/ppermute | solution.py:258
  147.4 1.1 slice_add_fusion
  148.5 2.2 %collective-permute-start.1 = (f32[4,16,2048]{2,1,0:T(8,128)S(1)}, f32[4,16,2048]{2,1,0:T(8,128)S(1)}, u32[]{:S(2)}, u32[]{:S(2)}) collective-permute-start(f32[4,16,2048]{2,1,0:T(8,128)S(1)} %slice_add_fusion), channel_id=1, source_target_pairs={{0,128},{64,192},{128,0},{192,64},{256,384},{320,448},{384,256},{4... | collective-permute-start | bytes 1572872 | tf_op jit(solution)/shard_map/ppermute | solution.py:261
  150.7 6.1 %all-to-all-start.6 = ((f32[64,6,256]{2,1,0:T(8,128)}), f32[64,6,256]{2,1,0:T(8,128)S(1)}, u32[]{:S(2)}, u32[]{:S(2)}) async-start(f32[64,6,256]{2,1,0:T(8,128)} %get-tuple-element.20), calls=%async_computation.6 | async-start | bytes 1048576 | tf_op jit(solution)/shard_map/all_to_all | solution.py:213
  156.9 7.5 %collective-permute-done.1 = f32[4,16,2048]{2,1,0:T(8,128)S(1)} collective-permute-done((f32[4,16,2048]{2,1,0:T(8,128)S(1)}, f32[4,16,2048]{2,1,0:T(8,128)S(1)}, u32[]{:S(2)}, u32[]{:S(2)}) %collective-permute-start.1) | collective-permute-done | bytes 524320 | tf_op jit(solution)/shard_map/ppermute | solution.py:261
  164.4 1.9 fusion
  166.3 10.2 %all-to-all-done.6 = f32[64,6,256]{2,1,0:T(8,128)S(1)} async-done(((f32[64,6,256]{2,1,0:T(8,128)}), f32[64,6,256]{2,1,0:T(8,128)S(1)}, u32[]{:S(2)}, u32[]{:S(2)}) %all-to-all-start.6) | async-done | bytes 393248 | tf_op jit(solution)/shard_map/all_to_all | solution.py:213
  176.5 3.5 %all-to-all-start.7 = ((f32[4,16,2048]{2,1,0:T(8,128)}), f32[4,16,2048]{2,1,0:T(8,128)S(1)}, u32[]{:S(2)}, u32[]{:S(2)}) async-start(f32[4,16,2048]{2,1,0:T(8,128)} %fusion), calls=%async_computation.7 | async-start | bytes 1048576 | tf_op jit(solution)/shard_map/all_to_all | solution.py:264
  180.0 0.8 multiply_reduce_fusion.1
  180.9 0.1 reduce_sum.37
  181.0 0.9 multiply_reduce_fusion
  181.9 1.4 subtract_multiply_fusion
  183.3 11.1 %all-to-all-done.7 = f32[4,16,2048]{2,1,0:T(8,128)S(1)} async-done(((f32[4,16,2048]{2,1,0:T(8,128)}), f32[4,16,2048]{2,1,0:T(8,128)S(1)}, u32[]{:S(2)}, u32[]{:S(2)}) %all-to-all-start.7) | async-done | bytes 524320 | tf_op jit(solution)/shard_map/all_to_all | solution.py:264
  194.3 0.7 reduce_sum.39
  (2 shorter events, 0.0 us)
Async XLA Ops:
  6.0 25.5 %all-to-all-start = ((f32[16,16,128]{2,1,0:T(8,128)}), f32[16,16,128]{2,1,0:T(8,128)S(1)}, u32[]{:S(2)}, u32[]{:S(2)}) async-start(f32[16,16,128]{2,1,0:T(8,128)} %get-tuple-element.14), calls=%async_computation | async-start | bytes 262144 | tf_op jit(solution)/shard_map/all_to_all | solution.py:213
  31.5 0.7 copy-start
  142.7 4.8 %collective-permute-start = (f32[8,16,2048]{2,1,0:T(8,128)}, f32[8,16,2048]{2,1,0:T(8,128)S(1)}, u32[]{:S(2)}, u32[]{:S(2)}) collective-permute-start(f32[8,16,2048]{2,1,0:T(8,128)} %get-tuple-element.22), channel_id=1, source_target_pairs={{0,64},{64,0},{128,192},{192,128},{256,320},{320,256},{384,448},{4... | collective-permute-start | bytes 3145736 | tf_op jit(solution)/shard_map/ppermute | solution.py:258
  148.5 15.9 %collective-permute-start.1 = (f32[4,16,2048]{2,1,0:T(8,128)S(1)}, f32[4,16,2048]{2,1,0:T(8,128)S(1)}, u32[]{:S(2)}, u32[]{:S(2)}) collective-permute-start(f32[4,16,2048]{2,1,0:T(8,128)S(1)} %slice_add_fusion), channel_id=1, source_target_pairs={{0,128},{64,192},{128,0},{192,64},{256,384},{320,448},{384,256},{4... | collective-permute-start | bytes 1572872 | tf_op jit(solution)/shard_map/ppermute | solution.py:261
  150.7 25.8 %all-to-all-start.6 = ((f32[64,6,256]{2,1,0:T(8,128)}), f32[64,6,256]{2,1,0:T(8,128)S(1)}, u32[]{:S(2)}, u32[]{:S(2)}) async-start(f32[64,6,256]{2,1,0:T(8,128)} %get-tuple-element.20), calls=%async_computation.6 | async-start | bytes 1048576 | tf_op jit(solution)/shard_map/all_to_all | solution.py:213
  176.5 17.8 %all-to-all-start.7 = ((f32[4,16,2048]{2,1,0:T(8,128)}), f32[4,16,2048]{2,1,0:T(8,128)S(1)}, u32[]{:S(2)}, u32[]{:S(2)}) async-start(f32[4,16,2048]{2,1,0:T(8,128)} %fusion), calls=%async_computation.7 | async-start | bytes 1048576 | tf_op jit(solution)/shard_map/all_to_all | solution.py:264
